TPU v7x, 32 devices: a whole 2x2x4 slice. The times are simulated.
32 devices in a mesh: seg: 8 (over z, y), ctl: 4 (over x, core).
Axes of the slice: x: 2, y: 2, z: 4, core: 2. Of those that a mesh axis runs over, the one named last changes fastest.
Arguments:
- transition: float32 [8, 1024, 1024], P('seg'), may hold values from -1 to 1
- control_map: float32 [8, 1024, 256], P('seg'), may hold values from -1.5 to 1.5
- weights: float32 [8, 1024], P('seg'), may hold values from 0.01 to 0.5
Outputs:
- sensitivity: float32 [8, 1024, 2048], P('seg', None, 'ctl')
- hessian_tiles: float32 [4, 512, 512], P('ctl', 'seg')
All inputs are finite; a program needn't handle non-finite values.
Results may differ from a plain program's by a relative error of at most 0.0003.
Values sent between devices are 32-bit elements; how exact they have to be, the bound alone decides.
No kernel may reach another device: no remote copies, remote signals or barrier semaphores. Data moves between devices by JAX's collectives and lax.ppermute only.
A program may use at most 128 MiB of HBM per device.

v0:
```python
import jax
import jax.numpy as jnp
from jax import lax
from jax.sharding import PartitionSpec as P


def from_behind(value, axis, by):
    devices = lax.axis_size(axis)
    pairs = [(i, i + by) for i in range(devices) if 0 <= i + by < devices]
    return lax.ppermute(value, axis, pairs)


def matmul_hi(left, right):
    return jnp.dot(left, right, precision=lax.Precision.HIGHEST, preferred_element_type=jnp.float32)


def gather_matrix(m_cols):
    return lax.all_gather(m_cols, "ctl", axis=1, tiled=True)


def earlier_sens(sens_block, reach):
    return from_behind(sens_block, "seg", reach)


def local(transition, control_map, weights):
    own_trans = transition[0]
    own_input = control_map[0]
    weight_row = weights[0]
    nseg = lax.axis_size("seg")
    nctl = lax.axis_size("ctl")
    seg_pos = lax.axis_index("seg")
    ctl_pos = lax.axis_index("ctl")
    stride = nseg // (2 * nctl)
    shard_width = own_trans.shape[1] // nctl
    blocks = [
        jnp.where(seg_pos == (2 * ctl_pos + slot_idx) * stride, own_input, 0.0)
        for slot_idx in range(2)
    ]
    sens_block = jnp.concatenate(blocks, axis=1)
    m_cols = lax.dynamic_slice_in_dim(own_trans, ctl_pos * shard_width, shard_width, 1)
    levels = (nseg - 1).bit_length()
    for level_idx in range(levels):
        reach = 1 << level_idx
        active = seg_pos >= reach
        is_last = level_idx == levels - 1
        own_whole = own_trans if level_idx == 0 else gather_matrix(m_cols)
        if is_last:
            prior_c = earlier_sens(sens_block, reach)
        else:
            prior_m, prior_c = from_behind((m_cols, sens_block), "seg", reach)
            m_cols = jnp.where(active, matmul_hi(own_whole, prior_m), m_cols)
        sens_block = jnp.where(active, matmul_hi(own_whole, prior_c) + sens_block, sens_block)
    weighted = sens_block * weight_row[:, None]
    hess_tile = lax.dot_general(
        sens_block,
        weighted,
        (((0,), (0,)), ((), ())),
        precision=lax.Precision.HIGHEST,
        preferred_element_type=jnp.float32,
    )
    summed = lax.psum(hess_tile, "seg")
    row_count = hess_tile.shape[0] // nseg
    hess_rows = lax.dynamic_slice_in_dim(summed, seg_pos * row_count, row_count, 0)
    return (sens_block[None], hess_rows[None])


def solution(mesh):
    return jax.shard_map(
        local,
        mesh=mesh,
        in_specs=(P("seg", None, None), P("seg", None, None), P("seg", None)),
        out_specs=(P("seg", None, "ctl"), P("ctl", "seg", None)),
        check_vma=False,
    )
```

profile of v0, /device:TPU:0, one launch (start us, length us, event | category | flops | bytes accessed | tf_op | source)
XLA Modules:
  0.0 375.8 jit_solution(13403189669114967752)
XLA Ops:
  7.2 0.0 all-gather.3.cloned.1.call-start
  7.2 1.3 constant_dynamic-slice_fusion
  8.5 0.3 copy.5
  8.9 5.0 %collective-permute-start = (f32[1024,256]{0,1:T(8,128)S(1)}, f32[1024,256]{0,1:T(8,128)S(1)}, u32[]{:S(2)}, u32[]{:S(2)}) collective-permute-start(f32[1024,256]{0,1:T(8,128)S(1)} %bitcast.37), channel_id=1, source_target_pairs={{0,4},{4,8},{8,12},{12,16},{16,20},{20,24},{24,28},{1,5},{5,9},{9,... | collective-permute-start | bytes 3145736 | tf_op jit(solution)/shard_map/ppermute | solution.py:10
  13.8 0.0 copy-start.3
  13.8 22.3 %collective-permute-done = f32[1024,256]{0,1:T(8,128)S(1)} collective-permute-done((f32[1024,256]{0,1:T(8,128)S(1)}, f32[1024,256]{0,1:T(8,128)S(1)}, u32[]{:S(2)}, u32[]{:S(2)}) %collective-permute-start) | collective-permute-done | bytes 1048608 | tf_op jit(solution)/shard_map/ppermute | solution.py:10
  36.2 6.9 %fusion.11 = f32[1024,256]{0,1:T(8,128)} fusion(f32[1024,256]{0,1:T(8,128)S(1)} %collective-permute-done, f32[1,1024,1024]{2,1,0:T(8,128)} %param.3, pred[]{:T(512)S(6)} %ge.11, f32[1,1024,256]{1,2,0:T(8,128)S(1)} %copy.5), kind=kOutput, calls=%fused_computation.11 | convolution fusion | flops 3221487616 | bytes 7340033 | tf_op jit(solution)/shard_map/dot_general | solution.py:14
  43.0 0.0 copy-start.1
  43.0 0.0 all-gather.3.cloned.1.call-update
  43.1 0.0 all-gather.5.cloned.1.call-start
  43.1 0.0 copy-done.3
  43.1 1.3 copy.6
  44.4 0.0 copy-done.1
  44.4 6.4 %collective-permute-start.1 = (f32[1024,256]{0,1:T(8,128)S(1)}, f32[1024,256]{0,1:T(8,128)}, u32[]{:S(2)}, u32[]{:S(2)}) collective-permute-start(f32[1024,256]{0,1:T(8,128)S(1)} %copy-done.1), channel_id=1, source_target_pairs={{0,8},{4,12},{8,16},{12,20},{16,24},{20,28},{1,9},{5,13},{9,17},{1... | collective-permute-start | bytes 3145736 | tf_op jit(solution)/shard_map/ppermute | solution.py:10
  50.8 1.6 select_bitcast_fusion.1
  52.4 1.5 pad_maximum_fusion
  53.8 3.8 %collective-permute-start.2 = (f32[1024,512]{0,1:T(8,128)}, f32[1024,512]{0,1:T(8,128)}, u32[]{:S(2)}, u32[]{:S(2)}) collective-permute-start(f32[1024,512]{0,1:T(8,128)} %pad_maximum_fusion), channel_id=1, source_target_pairs={{0,4},{4,8},{8,12},{12,16},{16,20},{20,24},{24,28},{1,5},{5,9},{9,... | collective-permute-start | bytes 6291464 | tf_op jit(solution)/shard_map/ppermute | solution.py:10
  57.6 13.7 %collective-permute-done.1 = f32[1024,256]{0,1:T(8,128)} collective-permute-done((f32[1024,256]{0,1:T(8,128)S(1)}, f32[1024,256]{0,1:T(8,128)}, u32[]{:S(2)}, u32[]{:S(2)}) %collective-permute-start.1) | collective-permute-done | bytes 1048608 | tf_op jit(solution)/shard_map/ppermute | solution.py:10
  71.3 8.6 %all-gather.3.cloned.1.call-done = f32[1024,1024]{0,1:T(8,128)} async-done(((f32[1024,256]{0,1:T(8,128)}), f32[1024,1024]{0,1:T(8,128)}) %all-gather.3.cloned.1.call-update) | async-done | bytes 4194320 | tf_op jit(solution)/shard_map/all_gather | solution.py:18
  79.9 7.3 %convolution_select_fusion = f32[1024,256]{0,1:T(8,128)} fusion(f32[1024,256]{0,1:T(8,128)S(1)} %copy-done.1, f32[1024,1024]{0,1:T(8,128)} %all-gather.3.cloned.1.call-done, f32[1024,256]{0,1:T(8,128)} %collective-permute-done.1, pred[]{:T(512)S(6)} %ge.10), kind=kOutput, calls=%fused_computation.12 | convolution fusion | flops 3221487616 | bytes 7340033 | tf_op jit(solution)/shard_map/dot_general | solution.py:14
  87.1 0.0 all-gather.5.cloned.1.call-update
  87.1 0.2 all-reduce.2.cloned.1.call-start
  87.4 12.9 %collective-permute-done.2 = f32[1024,512]{0,1:T(8,128)} collective-permute-done((f32[1024,512]{0,1:T(8,128)}, f32[1024,512]{0,1:T(8,128)}, u32[]{:S(2)}, u32[]{:S(2)}) %collective-permute-start.2) | collective-permute-done | bytes 2097184 | tf_op jit(solution)/shard_map/ppermute | solution.py:10
  100.3 0.0 copy-start
  100.3 10.0 %add_select_fusion.2 = f32[1024,512]{0,1:T(8,128)S(1)} fusion(f32[1024,512]{0,1:T(8,128)} %collective-permute-done.2, f32[1,1024,1024]{2,1,0:T(8,128)} %param.3, pred[]{:T(512)S(6)} %ge.11, f32[1024,256]{0,1:T(8,128)S(1)} %get-tuple-element.5, f32[1024,256]{0,1:T(8,128)S(1)} %get-tuple-element.4), kind=kOutput, calls=%fused_computation.8 | convolution fusion | flops 6444023808 | bytes 10485761 | tf_op jit(solution)/shard_map/dot_general | solution.py:14
  110.3 20.6 %collective-permute-start.3 = (f32[1024,512]{0,1:T(8,128)S(1)}, f32[1024,512]{0,1:T(8,128)S(1)}, u32[]{:S(2)}, u32[]{:S(2)}) collective-permute-start(f32[1024,512]{0,1:T(8,128)S(1)} %add_select_fusion.2), channel_id=1, source_target_pairs={{0,8},{4,12},{8,16},{12,20},{16,24},{20,28},{1,9},{5,13},{9,17},{1... | collective-permute-start | bytes 6291464 | tf_op jit(solution)/shard_map/ppermute | solution.py:10
  131.0 43.0 %collective-permute-done.3 = f32[1024,512]{0,1:T(8,128)S(1)} collective-permute-done((f32[1024,512]{0,1:T(8,128)S(1)}, f32[1024,512]{0,1:T(8,128)S(1)}, u32[]{:S(2)}, u32[]{:S(2)}) %collective-permute-start.3) | collective-permute-done | bytes 2097184 | tf_op jit(solution)/shard_map/ppermute | solution.py:10
  174.0 0.0 copy-done
  174.0 7.0 %add_select_fusion.1 = f32[1024,512]{0,1:T(8,128)S(1)} fusion(f32[1024,512]{0,1:T(8,128)S(1)} %add_select_fusion.2, f32[1024,1024]{0,1:T(8,128)S(1)} %copy-done, f32[1024,512]{0,1:T(8,128)S(1)} %collective-permute-done.3, pred[]{:T(512)S(6)} %ge.10), kind=kOutput, calls=%fused_computation.7 | convolution fusion | flops 6443499520 | bytes 10485761 | tf_op jit(solution)/shard_map/dot_general | solution.py:14
  180.9 0.0 copy-start.2
  180.9 6.8 %collective-permute-start.4 = (f32[1024,512]{0,1:T(8,128)S(1)}, f32[1024,512]{0,1:T(8,128)}, u32[]{:S(2)}, u32[]{:S(2)}) collective-permute-start(f32[1024,512]{0,1:T(8,128)S(1)} %add_select_fusion.1), channel_id=1, source_target_pairs={{0,16},{4,20},{8,24},{12,28},{1,17},{5,21},{9,25},{13,29},{2,18},{... | collective-permute-start | bytes 6291464 | tf_op jit(solution)/shard_map/ppermute | solution.py:10
  187.7 0.0 copy-start.4
  187.7 41.0 %collective-permute-done.4 = f32[1024,512]{0,1:T(8,128)} collective-permute-done((f32[1024,512]{0,1:T(8,128)S(1)}, f32[1024,512]{0,1:T(8,128)}, u32[]{:S(2)}, u32[]{:S(2)}) %collective-permute-start.4) | collective-permute-done | bytes 2097184 | tf_op jit(solution)/shard_map/ppermute | solution.py:10
  228.7 0.0 copy-done.2
  228.7 0.0 all-gather.5.cloned.1.call-done
  228.7 9.8 %add_select_fusion = f32[1024,512]{0,1:T(8,128)S(1)} fusion(f32[1024,512]{0,1:T(8,128)} %copy-done.2, f32[1024,1024]{0,1:T(8,128)} %all-gather.5.cloned.1.call-done, f32[1024,512]{0,1:T(8,128)} %collective-permute-done.4, pred[]{:T(512)S(6)} %ge.9), kind=kOutput, calls=%fused_computation.6 | convolution fusion | flops 6443499520 | bytes 10485761 | tf_op jit(solution)/shard_map/dot_general | solution.py:14
  238.5 0.0 copy-done.4
  238.5 4.5 %fusion.4 = f32[512,512]{1,0:T(8,128)} fusion(f32[1024,512]{0,1:T(8,128)S(1)} %add_select_fusion, f32[1024]{0:T(1024)S(1)} %bitcast.38), kind=kOutput, calls=%fused_computation.4 | convolution fusion | flops 3221749760 | bytes 3149824 | tf_op jit(solution)/shard_map/dot_general | solution.py:54
  243.1 0.0 all-reduce.2.cloned.1.call-update
  243.1 1.8 copy.10
  244.9 122.8 %all-reduce.2.cloned.1.call-done = f32[512,512]{1,0:T(8,128)} async-done(((f32[512,512]{1,0:T(8,128)}), f32[512,512]{1,0:T(8,128)}) %all-reduce.2.cloned.1.call-update) | async-done | bytes 1048592 | tf_op jit(solution)/shard_map/psum | solution.py:61
  367.7 1.6 dynamic-slice_bitcast_fusion
Async XLA Ops:
  7.2 72.7 %all-gather.3.cloned.1.call-start = ((), (), s32[]{:S(2)}) async-start(), calls=%async_computation | async-start | bytes 5242880 | tf_op jit(solution)/shard_map/all_gather | solution.py:18
  8.9 27.3 %collective-permute-start = (f32[1024,256]{0,1:T(8,128)S(1)}, f32[1024,256]{0,1:T(8,128)S(1)}, u32[]{:S(2)}, u32[]{:S(2)}) collective-permute-start(f32[1024,256]{0,1:T(8,128)S(1)} %bitcast.37), channel_id=1, source_target_pairs={{0,4},{4,8},{8,12},{12,16},{16,20},{20,24},{24,28},{1,5},{5,9},{9,... | collective-permute-start | bytes 3145736 | tf_op jit(solution)/shard_map/ppermute | solution.py:10
  13.8 29.3 %copy-start.3 = (f32[1,1024,256]{2,1,0:T(8,128)S(1)}, f32[1,1024,256]{2,1,0:T(8,128)}, u32[]{:S(2)}) copy-start(f32[1,1024,256]{2,1,0:T(8,128)} %param.4) | copy-start | bytes 3145732
  43.0 1.4 copy-start.1
  43.1 185.6 %all-gather.5.cloned.1.call-start = ((), (), s32[]{:S(2)}) async-start(), calls=%async_computation.1 | async-start | bytes 5242880 | tf_op jit(solution)/shard_map/all_gather | solution.py:18
  44.4 26.9 %collective-permute-start.1 = (f32[1024,256]{0,1:T(8,128)S(1)}, f32[1024,256]{0,1:T(8,128)}, u32[]{:S(2)}, u32[]{:S(2)}) collective-permute-start(f32[1024,256]{0,1:T(8,128)S(1)} %copy-done.1), channel_id=1, source_target_pairs={{0,8},{4,12},{8,16},{12,20},{16,24},{20,28},{1,9},{5,13},{9,17},{1... | collective-permute-start | bytes 3145736 | tf_op jit(solution)/shard_map/ppermute | solution.py:10
  53.8 46.5 %collective-permute-start.2 = (f32[1024,512]{0,1:T(8,128)}, f32[1024,512]{0,1:T(8,128)}, u32[]{:S(2)}, u32[]{:S(2)}) collective-permute-start(f32[1024,512]{0,1:T(8,128)} %pad_maximum_fusion), channel_id=1, source_target_pairs={{0,4},{4,8},{8,12},{12,16},{16,20},{20,24},{24,28},{1,5},{5,9},{9,... | collective-permute-start | bytes 6291464 | tf_op jit(solution)/shard_map/ppermute | solution.py:10
  87.1 280.6 %all-reduce.2.cloned.1.call-start = ((), (), s32[]{:S(2)}) async-start(), calls=%async_computation.2 | async-start | bytes 2097152 | tf_op jit(solution)/shard_map/psum | solution.py:61
  100.3 73.7 %copy-start = (f32[1024,1024]{0,1:T(8,128)S(1)}, f32[1024,1024]{0,1:T(8,128)}, u32[]{:S(2)}) copy-start(f32[1024,1024]{0,1:T(8,128)} %all-gather.3.cloned.1.call-done) | copy-start | bytes 12582916
  110.3 63.6 %collective-permute-start.3 = (f32[1024,512]{0,1:T(8,128)S(1)}, f32[1024,512]{0,1:T(8,128)S(1)}, u32[]{:S(2)}, u32[]{:S(2)}) collective-permute-start(f32[1024,512]{0,1:T(8,128)S(1)} %add_select_fusion.2), channel_id=1, source_target_pairs={{0,8},{4,12},{8,16},{12,20},{16,24},{20,28},{1,9},{5,13},{9,17},{1... | collective-permute-start | bytes 6291464 | tf_op jit(solution)/shard_map/ppermute | solution.py:10
  180.9 47.7 %copy-start.2 = (f32[1024,512]{0,1:T(8,128)}, f32[1024,512]{0,1:T(8,128)S(1)}, u32[]{:S(2)}) copy-start(f32[1024,512]{0,1:T(8,128)S(1)} %add_select_fusion.1) | copy-start | bytes 6291460
  180.9 47.7 %collective-permute-start.4 = (f32[1024,512]{0,1:T(8,128)S(1)}, f32[1024,512]{0,1:T(8,128)}, u32[]{:S(2)}, u32[]{:S(2)}) collective-permute-start(f32[1024,512]{0,1:T(8,128)S(1)} %add_select_fusion.1), channel_id=1, source_target_pairs={{0,16},{4,20},{8,24},{12,28},{1,17},{5,21},{9,25},{13,29},{2,18},{... | collective-permute-start | bytes 6291464 | tf_op jit(solution)/shard_map/ppermute | solution.py:10
  187.7 50.8 %copy-start.4 = (f32[1,1024]{1,0:T(1,128)S(1)}, f32[1,1024]{1,0:T(1,128)}, u32[]{:S(2)}) copy-start(f32[1,1024]{1,0:T(1,128)} %param.5) | copy-start | bytes 12292
Sparse Core Ops, SparseCore 0:
  43.2 36.6 all-gather.2
  87.3 34.4 all-gather.4
  243.2 124.4 all-reduce.1
where the time goes:
time: 376 us
  waiting for transfers between devices  264 us (70%)
  matrix products  45.5 us (12%)
  starting transfers between devices  42.8 us (11%)
  between operations  13.9 us (4%)
  local copies, waits for them, and re-layouts  6.34 us (2%)
    ppermute x5, waiting for transfers between devices, from_behind(): return lax.ppermute(value, axis, pairs)  133 us
    psum x1, waiting for transfers between devices, local(): summed = lax.psum(hess_tile, 'seg')  123 us
    ppermute x5, starting transfers between devices, from_behind(): return lax.ppermute(value, axis, pairs)  42.5 us
    dot_general x5, matrix products, matmul_hi(): jnp.dot(left, right, precision=lax.Precision.HIGHEST, preferred_element_t...  40.9 us
    all_gather x2, waiting for transfers between devices, gather_matrix(): return lax.all_gather(m_cols, 'ctl', axis=1, tiled=True)  8.56 us
  transfers between devices with their start and end apart: 8, of which 7 were waited for; matrix products, arithmetic and copies ran while one was open for 8% of the time, Pallas kernels for 0%

commit v1 on v0

--- a/solution.py
+++ b/solution.py
@@ -58,7 +58,8 @@
         precision=lax.Precision.HIGHEST,
         preferred_element_type=jnp.float32,
     )
-    summed = lax.psum(hess_tile, "seg")
+    pieces = lax.all_gather(hess_tile, "seg")
+    summed = jnp.sum(pieces, axis=0)
     row_count = hess_tile.shape[0] // nseg
     hess_rows = lax.dynamic_slice_in_dim(summed, seg_pos * row_count, row_count, 0)
     return (sens_block[None], hess_rows[None])

time: 376 us -> 426 us (1.13)
  waiting for transfers between devices: 264 us -> 310 us
  other arithmetic: 3.03 us -> 7.52 us
    all_gather x0 -> x1, waiting for transfers between devices: none -> 169 us  [local(): pieces = lax.all_gather(hess_tile, 'seg')]
    psum x1 -> x0, waiting for transfers between devices: 123 us -> none  [local(): summed = lax.psum(hess_tile, 'seg')]
    reduce_sum x0 -> x1, other arithmetic: none -> 4.49 us  [local(): summed = jnp.sum(pieces, axis=0)]
  transfers between devices with their start and end apart: 8 -> 8, of which waited for: 7 -> 7; matrix products, arithmetic and copies ran while one was open for 8% -> 7% of each run, Pallas kernels for 0% -> 0%
where the time goes in v1:
time: 426 us
  waiting for transfers between devices  310 us (73%)
  matrix products  45.5 us (11%)
  starting transfers between devices  42.8 us (10%)
  between operations  13.9 us (3%)
  other arithmetic  7.52 us (2%)
  local copies, waits for them, and re-layouts  5.45 us (1%)
    all_gather x1, waiting for transfers between devices, local(): pieces = lax.all_gather(hess_tile, 'seg')  169 us
    ppermute x5, waiting for transfers between devices, from_behind(): return lax.ppermute(value, axis, pairs)  133 us
    ppermute x5, starting transfers between devices, from_behind(): return lax.ppermute(value, axis, pairs)  42.5 us
    dot_general x5, matrix products, matmul_hi(): jnp.dot(left, right, precision=lax.Precision.HIGHEST, preferred_element_t...  40.9 us
    all_gather x2, waiting for transfers between devices, gather_matrix(): return lax.all_gather(m_cols, 'ctl', axis=1, tiled=True)  8.56 us
  transfers between devices with their start and end apart: 8, of which 7 were waited for; matrix products, arithmetic and copies ran while one was open for 7% of the time, Pallas kernels for 0%

profile of v1, /device:TPU:0, one launch (start us, length us, event | category | flops | bytes accessed | tf_op | source)
XLA Modules:
  0.0 425.6 jit_solution(9076052671332446366)
XLA Ops:
  7.2 0.0 all-gather.5.cloned.1.call-start
  7.2 1.3 constant_dynamic-slice_fusion
  8.5 0.3 copy.5
  8.9 5.0 %collective-permute-start = (f32[1024,256]{0,1:T(8,128)S(1)}, f32[1024,256]{0,1:T(8,128)S(1)}, u32[]{:S(2)}, u32[]{:S(2)}) collective-permute-start(f32[1024,256]{0,1:T(8,128)S(1)} %bitcast.39), channel_id=1, source_target_pairs={{0,4},{4,8},{8,12},{12,16},{16,20},{20,24},{24,28},{1,5},{5,9},{9,... | collective-permute-start | bytes 3145736 | tf_op jit(solution)/shard_map/ppermute | solution.py:10
  13.8 0.0 copy-start.3
  13.8 22.3 %collective-permute-done = f32[1024,256]{0,1:T(8,128)S(1)} collective-permute-done((f32[1024,256]{0,1:T(8,128)S(1)}, f32[1024,256]{0,1:T(8,128)S(1)}, u32[]{:S(2)}, u32[]{:S(2)}) %collective-permute-start) | collective-permute-done | bytes 1048608 | tf_op jit(solution)/shard_map/ppermute | solution.py:10
  36.2 6.9 %fusion.11 = f32[1024,256]{0,1:T(8,128)} fusion(f32[1024,256]{0,1:T(8,128)S(1)} %collective-permute-done, f32[1,1024,1024]{2,1,0:T(8,128)} %param.3, pred[]{:T(512)S(6)} %ge.11, f32[1,1024,256]{1,2,0:T(8,128)S(1)} %copy.5), kind=kOutput, calls=%fused_computation.11 | convolution fusion | flops 3221487616 | bytes 7340033 | tf_op jit(solution)/shard_map/dot_general | solution.py:14
  43.0 0.0 copy-start.1
  43.0 0.0 all-gather.5.cloned.1.call-update
  43.1 0.0 all-gather.7.cloned.1.call-start
  43.1 0.0 copy-done.3
  43.1 1.3 copy.6
  44.4 0.0 copy-done.1
  44.4 6.4 %collective-permute-start.1 = (f32[1024,256]{0,1:T(8,128)S(1)}, f32[1024,256]{0,1:T(8,128)}, u32[]{:S(2)}, u32[]{:S(2)}) collective-permute-start(f32[1024,256]{0,1:T(8,128)S(1)} %copy-done.1), channel_id=1, source_target_pairs={{0,8},{4,12},{8,16},{12,20},{16,24},{20,28},{1,9},{5,13},{9,17},{1... | collective-permute-start | bytes 3145736 | tf_op jit(solution)/shard_map/ppermute | solution.py:10
  50.8 1.6 select_bitcast_fusion.1
  52.4 1.5 pad_maximum_fusion
  53.8 3.8 collective-permute-start.2
  57.6 13.7 %collective-permute-done.1 = f32[1024,256]{0,1:T(8,128)} collective-permute-done((f32[1024,256]{0,1:T(8,128)S(1)}, f32[1024,256]{0,1:T(8,128)}, u32[]{:S(2)}, u32[]{:S(2)}) %collective-permute-start.1) | collective-permute-done | bytes 1048608 | tf_op jit(solution)/shard_map/ppermute | solution.py:10
  71.3 8.6 %all-gather.5.cloned.1.call-done = f32[1024,1024]{0,1:T(8,128)} async-done(((f32[1024,256]{0,1:T(8,128)}), f32[1024,1024]{0,1:T(8,128)}) %all-gather.5.cloned.1.call-update) | async-done | bytes 4194320 | tf_op jit(solution)/shard_map/all_gather | solution.py:18
  79.9 7.3 %convolution_select_fusion = f32[1024,256]{0,1:T(8,128)} fusion(f32[1024,256]{0,1:T(8,128)S(1)} %copy-done.1, f32[1024,1024]{0,1:T(8,128)} %all-gather.5.cloned.1.call-done, f32[1024,256]{0,1:T(8,128)} %collective-permute-done.1, pred[]{:T(512)S(6)} %ge.10), kind=kOutput, calls=%fused_computation.12 | convolution fusion | flops 3221487616 | bytes 7340033 | tf_op jit(solution)/shard_map/dot_general | solution.py:14
  87.1 0.0 all-gather.7.cloned.1.call-update
  87.1 0.2 all-gather.9.cloned.1.call-start
  87.4 12.9 %collective-permute-done.2 = f32[1024,512]{0,1:T(8,128)} collective-permute-done((f32[1024,512]{0,1:T(8,128)}, f32[1024,512]{0,1:T(8,128)}, u32[]{:S(2)}, u32[]{:S(2)}) %collective-permute-start.2) | collective-permute-done | bytes 2097184 | tf_op jit(solution)/shard_map/ppermute | solution.py:10
  100.3 0.0 copy-start
  100.3 10.0 %add_select_fusion.2 = f32[1024,512]{0,1:T(8,128)S(1)} fusion(f32[1024,512]{0,1:T(8,128)} %collective-permute-done.2, f32[1,1024,1024]{2,1,0:T(8,128)} %param.3, pred[]{:T(512)S(6)} %ge.11, f32[1024,256]{0,1:T(8,128)S(1)} %get-tuple-element.5, f32[1024,256]{0,1:T(8,128)S(1)} %get-tuple-element.4), kind=kOutput, calls=%fused_computation.8 | convolution fusion | flops 6444023808 | bytes 10485761 | tf_op jit(solution)/shard_map/dot_general | solution.py:14
  110.3 20.6 %collective-permute-start.3 = (f32[1024,512]{0,1:T(8,128)S(1)}, f32[1024,512]{0,1:T(8,128)S(1)}, u32[]{:S(2)}, u32[]{:S(2)}) collective-permute-start(f32[1024,512]{0,1:T(8,128)S(1)} %add_select_fusion.2), channel_id=1, source_target_pairs={{0,8},{4,12},{8,16},{12,20},{16,24},{20,28},{1,9},{5,13},{9,17},{1... | collective-permute-start | bytes 6291464 | tf_op jit(solution)/shard_map/ppermute | solution.py:10
  131.0 43.0 %collective-permute-done.3 = f32[1024,512]{0,1:T(8,128)S(1)} collective-permute-done((f32[1024,512]{0,1:T(8,128)S(1)}, f32[1024,512]{0,1:T(8,128)S(1)}, u32[]{:S(2)}, u32[]{:S(2)}) %collective-permute-start.3) | collective-permute-done | bytes 2097184 | tf_op jit(solution)/shard_map/ppermute | solution.py:10
  174.0 0.0 copy-done
  174.0 7.0 %add_select_fusion.1 = f32[1024,512]{0,1:T(8,128)S(1)} fusion(f32[1024,512]{0,1:T(8,128)S(1)} %add_select_fusion.2, f32[1024,1024]{0,1:T(8,128)S(1)} %copy-done, f32[1024,512]{0,1:T(8,128)S(1)} %collective-permute-done.3, pred[]{:T(512)S(6)} %ge.10), kind=kOutput, calls=%fused_computation.7 | convolution fusion | flops 6443499520 | bytes 10485761 | tf_op jit(solution)/shard_map/dot_general | solution.py:14
  180.9 0.0 copy-start.2
  180.9 6.8 %collective-permute-start.4 = (f32[1024,512]{0,1:T(8,128)S(1)}, f32[1024,512]{0,1:T(8,128)}, u32[]{:S(2)}, u32[]{:S(2)}) collective-permute-start(f32[1024,512]{0,1:T(8,128)S(1)} %add_select_fusion.1), channel_id=1, source_target_pairs={{0,16},{4,20},{8,24},{12,28},{1,17},{5,21},{9,25},{13,29},{2,18},{... | collective-permute-start | bytes 6291464 | tf_op jit(solution)/shard_map/ppermute | solution.py:10
  187.7 0.0 copy-start.4
  187.7 41.0 %collective-permute-done.4 = f32[1024,512]{0,1:T(8,128)} collective-permute-done((f32[1024,512]{0,1:T(8,128)S(1)}, f32[1024,512]{0,1:T(8,128)}, u32[]{:S(2)}, u32[]{:S(2)}) %collective-permute-start.4) | collective-permute-done | bytes 2097184 | tf_op jit(solution)/shard_map/ppermute | solution.py:10
  228.7 0.0 copy-done.2
  228.7 0.0 all-gather.7.cloned.1.call-done
  228.7 9.8 %add_select_fusion = f32[1024,512]{0,1:T(8,128)S(1)} fusion(f32[1024,512]{0,1:T(8,128)} %copy-done.2, f32[1024,1024]{0,1:T(8,128)} %all-gather.7.cloned.1.call-done, f32[1024,512]{0,1:T(8,128)} %collective-permute-done.4, pred[]{:T(512)S(6)} %ge.9), kind=kOutput, calls=%fused_computation.6 | convolution fusion | flops 6443499520 | bytes 10485761 | tf_op jit(solution)/shard_map/dot_general | solution.py:14
  238.5 0.0 copy-done.4
  238.5 4.6 %fusion.4 = f32[512,512]{1,0:T(8,128)} fusion(f32[1024,512]{0,1:T(8,128)S(1)} %add_select_fusion, f32[1024]{0:T(1024)S(1)} %bitcast.40), kind=kOutput, calls=%fused_computation.4 | convolution fusion | flops 3221749760 | bytes 3149824 | tf_op jit(solution)/shard_map/dot_general | solution.py:54
  243.1 0.0 all-gather.9.cloned.1.call-update
  243.1 1.8 copy.10
  245.0 168.9 %all-gather.9.cloned.1.call-done = f32[4096,512]{1,0:T(8,128)} async-done(((f32[512,512]{1,0:T(8,128)}), f32[4096,512]{1,0:T(8,128)}) %all-gather.9.cloned.1.call-update) | async-done | bytes 8388624 | tf_op jit(solution)/shard_map/all_gather | solution.py:61
  413.9 4.5 %reduce_sum.9 = f32[512,512]{1,0:T(8,128)S(1)} reduce(f32[8,512,512]{2,1,0:T(8,128)} %bitcast.38, f32[]{:T(128)} %constant.25.clone.1), dimensions={0}, to_apply=%region_0.1 | reduce | flops 1835008 | bytes 9437188 | tf_op jit(solution)/shard_map/reduce_sum | solution.py:62
  418.4 0.7 dynamic-slice_bitcast_fusion
Async XLA Ops:
  7.2 72.7 %all-gather.5.cloned.1.call-start = ((), (), s32[]{:S(2)}) async-start(), calls=%async_computation | async-start | bytes 5242880 | tf_op jit(solution)/shard_map/all_gather | solution.py:18
  8.9 27.3 %collective-permute-start = (f32[1024,256]{0,1:T(8,128)S(1)}, f32[1024,256]{0,1:T(8,128)S(1)}, u32[]{:S(2)}, u32[]{:S(2)}) collective-permute-start(f32[1024,256]{0,1:T(8,128)S(1)} %bitcast.39), channel_id=1, source_target_pairs={{0,4},{4,8},{8,12},{12,16},{16,20},{20,24},{24,28},{1,5},{5,9},{9,... | collective-permute-start | bytes 3145736 | tf_op jit(solution)/shard_map/ppermute | solution.py:10
  13.8 29.3 %copy-start.3 = (f32[1,1024,256]{2,1,0:T(8,128)S(1)}, f32[1,1024,256]{2,1,0:T(8,128)}, u32[]{:S(2)}) copy-start(f32[1,1024,256]{2,1,0:T(8,128)} %param.4) | copy-start | bytes 3145732
  43.0 1.4 copy-start.1
  43.1 185.6 %all-gather.7.cloned.1.call-start = ((), (), s32[]{:S(2)}) async-start(), calls=%async_computation.1 | async-start | bytes 5242880 | tf_op jit(solution)/shard_map/all_gather | solution.py:18
  44.4 26.9 %collective-permute-start.1 = (f32[1024,256]{0,1:T(8,128)S(1)}, f32[1024,256]{0,1:T(8,128)}, u32[]{:S(2)}, u32[]{:S(2)}) collective-permute-start(f32[1024,256]{0,1:T(8,128)S(1)} %copy-done.1), channel_id=1, source_target_pairs={{0,8},{4,12},{8,16},{12,20},{16,24},{20,28},{1,9},{5,13},{9,17},{1... | collective-permute-start | bytes 3145736 | tf_op jit(solution)/shard_map/ppermute | solution.py:10
  53.8 46.5 %collective-permute-start.2 = (f32[1024,512]{0,1:T(8,128)}, f32[1024,512]{0,1:T(8,128)}, u32[]{:S(2)}, u32[]{:S(2)}) collective-permute-start(f32[1024,512]{0,1:T(8,128)} %pad_maximum_fusion), channel_id=1, source_target_pairs={{0,4},{4,8},{8,12},{12,16},{16,20},{20,24},{24,28},{1,5},{5,9},{9,... | collective-permute-start | bytes 6291464 | tf_op jit(solution)/shard_map/ppermute | solution.py:10
  87.1 326.7 %all-gather.9.cloned.1.call-start = ((), (), s32[]{:S(2)}) async-start(), calls=%async_computation.2 | async-start | bytes 9437184 | tf_op jit(solution)/shard_map/all_gather | solution.py:61
  100.3 73.7 %copy-start = (f32[1024,1024]{0,1:T(8,128)S(1)}, f32[1024,1024]{0,1:T(8,128)}, u32[]{:S(2)}) copy-start(f32[1024,1024]{0,1:T(8,128)} %all-gather.5.cloned.1.call-done) | copy-start | bytes 12582916
  110.3 63.6 %collective-permute-start.3 = (f32[1024,512]{0,1:T(8,128)S(1)}, f32[1024,512]{0,1:T(8,128)S(1)}, u32[]{:S(2)}, u32[]{:S(2)}) collective-permute-start(f32[1024,512]{0,1:T(8,128)S(1)} %add_select_fusion.2), channel_id=1, source_target_pairs={{0,8},{4,12},{8,16},{12,20},{16,24},{20,28},{1,9},{5,13},{9,17},{1... | collective-permute-start | bytes 6291464 | tf_op jit(solution)/shard_map/ppermute | solution.py:10
  180.9 47.7 %copy-start.2 = (f32[1024,512]{0,1:T(8,128)}, f32[1024,512]{0,1:T(8,128)S(1)}, u32[]{:S(2)}) copy-start(f32[1024,512]{0,1:T(8,128)S(1)} %add_select_fusion.1) | copy-start | bytes 6291460
  180.9 47.7 %collective-permute-start.4 = (f32[1024,512]{0,1:T(8,128)S(1)}, f32[1024,512]{0,1:T(8,128)}, u32[]{:S(2)}, u32[]{:S(2)}) collective-permute-start(f32[1024,512]{0,1:T(8,128)S(1)} %add_select_fusion.1), channel_id=1, source_target_pairs={{0,16},{4,20},{8,24},{12,28},{1,17},{5,21},{9,25},{13,29},{2,18},{... | collective-permute-start | bytes 6291464 | tf_op jit(solution)/shard_map/ppermute | solution.py:10
  187.7 50.8 %copy-start.4 = (f32[1,1024]{1,0:T(1,128)S(1)}, f32[1,1024]{1,0:T(1,128)}, u32[]{:S(2)}) copy-start(f32[1,1024]{1,0:T(1,128)} %param.5) | copy-start | bytes 12292
Sparse Core Ops, SparseCore 0:
  43.2 36.6 all-gather.4
  87.3 34.4 all-gather.6
  243.3 170.5 all-gather.8
